TPU v7x, 128 devices: a whole 4x4x4 slice. The times are simulated.
128 devices in a mesh: row: 8 (over y, core), col: 16 (over z, x).
Axes of the slice: x: 4, y: 4, z: 4, core: 2. Of those that a mesh axis runs over, the one named last changes fastest.
Arguments:
- hidden_states: bfloat16 [1024, 2048], P('col', 'row'), may hold values from -20 to 20
- input_gain: float32 [2, 2048], P(None, 'row'), may hold values from 0.25 to 1.75
- inner_weight: bfloat16 [2, 2048, 2, 4096], P(None, 'row', None, 'col'), may hold values from -0.125 to 0.125
- proj_weight: bfloat16 [2, 2048, 256], P(None, 'row'), may hold values from -0.125 to 0.125
- step_weight: bfloat16 [2, 2048, 64], P(None, 'row', 'col'), may hold values from -0.125 to 0.125
- inner_kernel: float32 [2, 4, 4096], P(None, None, 'col'), may hold values from -3 to 3
- proj_kernel: float32 [2, 4, 256], replicated, may hold values from -3 to 3
- step_bias: float32 [2, 64], P(None, 'col'), may hold values from -5 to -1
- decay_log: float32 [2, 64], P(None, 'col'), may hold values from -2 to 1
- skip_gain: float32 [2, 64], P(None, 'col'), may hold values from 0.5 to 1.5
- norm_gain: float32 [2, 4096], P(None, 'col'), may hold values from 0.25 to 1.75
- out_weight: bfloat16 [2, 4096, 2048], P(None, 'col', 'row'), may hold values from -0.09375 to 0.09375
- inner_cache: bfloat16 [2, 64, 3, 4096], P(None, 'row', None, 'col'), may hold values from -6 to 6
- proj_cache: bfloat16 [2, 64, 3, 256], P(None, 'row'), may hold values from -6 to 6
- state_cache: float32 [2, 64, 64, 64, 128], P(None, 'row', 'col'), may hold values from -1.2 to 1.2
- accepted: int32 [64], P('row'), may hold values from 1 to 16
- owners: int32 [64], P('row'), may hold values from 0 to 15, as said below
- tenant_ranges: int32 [4, 2], replicated, may hold values from 0 to 64, as said below
Outputs:
- hidden_output: bfloat16 [1024, 2048], P('col', 'row')
- step_states: bfloat16 [2, 64, 16, 64, 64, 128], P(None, 'row', None, 'col')
- owned_states: bfloat16 [8, 16, 2, 2, 64, 64, 128], P('row', 'col')
Inputs may be any that keep to these rules, and one draw needn't show every extreme that they name: `owners`: within the requests of one index of row (aligned blocks of 8) no owner appears more than 2 times, and in every block some owner appears exactly 2 times. `tenant_ranges`: the ranges are in order, disjoint and not empty; exactly 8 requests lie in no range.
All inputs are finite; a program needn't handle non-finite values.
Results may differ from a plain program's by a relative error of at most 0.024.
Values may be sent and summed in bfloat16 or wider, within the bound.
No kernel may reach another device: no remote copies, remote signals or barrier semaphores. Data moves between devices by JAX's collectives and lax.ppermute only.
A program may use at most 128 MiB of HBM per device.

v0:
```python
import jax
import jax.numpy as jnp
from jax import lax
from jax.sharding import PartitionSpec as P

S = 16
SEND_CAP = 2
EPSILON = 1e-05


def conv_silu(prefix, incoming, kernel):
    joined = jnp.concatenate([prefix, incoming], axis=1)
    length = incoming.shape[1]
    summed = joined[:, 0:length, :] * kernel[0]
    for offset in range(1, kernel.shape[0]):
        summed = summed + joined[:, offset : offset + length, :] * kernel[offset]
    return jax.nn.silu(summed)


def ssm_scan(decays, deltas, inner_values, b_values, c_values, skip_values, start_state):

    def advance(carried, packed):
        decay_now, delta_now, value_now, b_now, c_now = packed
        updated = (
            decay_now[:, :, None, None] * carried
            + (delta_now[:, :, None] * value_now)[:, :, :, None] * b_now[:, None, None, :]
        )
        output = (
            jnp.einsum("rhpn,rn->rhp", updated, c_now, precision=lax.Precision.HIGHEST)
            + skip_values[None, :, None] * value_now
        )
        return (updated, (output, updated.astype(jnp.bfloat16)))

    time_major = tuple(
        (
            jnp.moveaxis(member, 1, 0)
            for member in (decays, deltas, inner_values, b_values, c_values)
        )
    )
    last_state, (outputs, states) = lax.scan(advance, start_state, time_major)
    return (jnp.moveaxis(outputs, 0, 1), jnp.moveaxis(states, 0, 1))


def local(
    hidden_states,
    input_gain,
    inner_weight,
    proj_weight,
    step_weight,
    inner_kernel,
    proj_kernel,
    step_bias,
    decay_log,
    skip_gain,
    norm_gain,
    out_weight,
    inner_cache,
    proj_cache,
    state_cache,
    accepted,
    owners,
    tenant_ranges,
):
    layer_count = inner_weight.shape[0]
    row_width = inner_weight.shape[1]
    inner_local = inner_weight.shape[3]
    heads_local = step_weight.shape[2]
    head_size = inner_local // heads_local
    state_size = proj_weight.shape[2] // 2
    requests_local = state_cache.shape[1]
    draft_steps = S
    row_count = lax.axis_size("row")
    col_count = lax.axis_size("col")
    model_width = row_width * row_count
    inner_width = inner_local * col_count
    token_rows = requests_local * draft_steps
    local_ids = jnp.arange(requests_local, dtype=jnp.int32)
    request_ids = lax.axis_index("row") * requests_local + local_ids
    live_mask = jnp.any(
        (request_ids[:, None] >= tenant_ranges[None, :, 0])
        & (request_ids[:, None] < tenant_ranges[None, :, 1]),
        axis=1,
    )
    earlier = (owners[:, None] == owners[None, :]) & (local_ids[None, :] < local_ids[:, None])
    slot_ranks = jnp.sum(earlier.astype(jnp.int32), axis=1)
    slot_ids = owners * SEND_CAP + slot_ranks
    slot_grid = jnp.arange(col_count * SEND_CAP, dtype=jnp.int32)
    step_grid = jnp.arange(draft_steps, dtype=jnp.int32)
    picker = (
        (slot_grid[:, None, None] == slot_ids[None, :, None])
        & (step_grid[None, None, :] == accepted[None, :, None] - 1)
        & live_mask[None, :, None]
    )
    picker = picker.astype(jnp.bfloat16).reshape(col_count * SEND_CAP, token_rows)
    hidden = hidden_states
    step_outputs = []
    chosen_layers = []
    for layer_index in range(layer_count):
        all_tokens = lax.all_gather(hidden, "col", axis=0, tiled=True)
        tokens_f = all_tokens.astype(jnp.float32)
        scaled = (tokens_f * input_gain[layer_index]).astype(jnp.bfloat16)
        square_part = jnp.sum(tokens_f * tokens_f, axis=1)
        inner_part = jnp.dot(
            scaled,
            inner_weight[layer_index].reshape(row_width, 2 * inner_local),
            preferred_element_type=jnp.float32,
        )
        step_part = jnp.dot(scaled, step_weight[layer_index], preferred_element_type=jnp.float32)
        proj_part = jnp.dot(scaled, proj_weight[layer_index], preferred_element_type=jnp.float32)
        inner_sum, step_sum, proj_sum, square_sum = (
            lax.psum_scatter(inner_part, "row", scatter_dimension=0, tiled=True),
            lax.psum_scatter(step_part, "row", scatter_dimension=0, tiled=True),
            lax.psum_scatter(proj_part, "row", scatter_dimension=0, tiled=True),
            lax.psum_scatter(square_part, "row", scatter_dimension=0, tiled=True),
        )
        inverse_rms = lax.rsqrt(square_sum / model_width + EPSILON)
        inner_vals = inner_sum * inverse_rms[:, None]
        gate_vals = inner_vals[:, :inner_local]
        raw_inner = inner_vals[:, inner_local:].reshape(requests_local, draft_steps, inner_local)
        raw_proj = (proj_sum * inverse_rms[:, None]).reshape(
            requests_local, draft_steps, 2 * state_size
        )
        conv_inner = conv_silu(
            inner_cache[layer_index].astype(jnp.float32), raw_inner, inner_kernel[layer_index]
        )
        conv_proj = conv_silu(
            proj_cache[layer_index].astype(jnp.float32), raw_proj, proj_kernel[layer_index]
        )
        deltas = jax.nn.softplus(
            (step_sum * inverse_rms[:, None]).reshape(requests_local, draft_steps, heads_local)
            + step_bias[layer_index]
        )
        decays = jnp.exp(-deltas * jnp.exp(decay_log[layer_index]))
        outputs, states = ssm_scan(
            decays,
            deltas,
            conv_inner.reshape(requests_local, draft_steps, heads_local, head_size),
            conv_proj[..., :state_size],
            conv_proj[..., state_size:],
            skip_gain[layer_index],
            state_cache[layer_index],
        )
        step_outputs.append(states)
        gated_raw = outputs.reshape(token_rows, inner_local) * jax.nn.silu(gate_vals)
        gate_square = lax.psum(jnp.sum(gated_raw * gated_raw, axis=1), "col")
        gated = (
            gated_raw
            * norm_gain[layer_index]
            * lax.rsqrt(gate_square / inner_width + EPSILON)[:, None]
        ).astype(jnp.bfloat16)
        layer_weight = out_weight[layer_index]
        partial_out = jnp.dot(
            lax.all_gather(gated, "row", axis=0, tiled=True),
            layer_weight,
            preferred_element_type=jnp.float32,
        )
        out_sum = lax.psum_scatter(
            partial_out.astype(jnp.bfloat16), "col", scatter_dimension=0, tiled=True
        ).astype(jnp.float32)
        hidden = (hidden.astype(jnp.float32) + out_sum).astype(jnp.bfloat16)
        chosen = jnp.dot(
            picker,
            states.reshape(token_rows, heads_local * head_size * state_size),
            preferred_element_type=jnp.float32,
        )
        chosen = chosen.astype(jnp.bfloat16).reshape(
            col_count, SEND_CAP, heads_local, head_size, state_size
        )
        chosen_layers.append(chosen)
    gathered = lax.all_to_all(
        jnp.stack(chosen_layers, axis=2), "col", split_axis=0, concat_axis=3, tiled=True
    )
    owned_block = gathered[None]
    step_all = jnp.stack(step_outputs, axis=0)
    return (hidden, step_all, owned_block)


def solution(mesh):
    placed = (
        P("col", "row"),
        P(None, "row"),
        P(None, "row", None, "col"),
        P(None, "row", None),
        P(None, "row", "col"),
        P(None, None, "col"),
        P(),
        P(None, "col"),
        P(None, "col"),
        P(None, "col"),
        P(None, "col"),
        P(None, "col", "row"),
        P(None, "row", None, "col"),
        P(None, "row", None, None),
        P(None, "row", "col", None, None),
        P("row"),
        P("row"),
        P(),
    )
    return jax.shard_map(
        local,
        mesh=mesh,
        in_specs=placed,
        out_specs=(
            P("col", "row"),
            P(None, "row", None, "col", None, None),
            P("row", "col", None, None, None, None, None),
        ),
        check_vma=False,
    )
```

profile of v0, /device:TPU:0, one launch (start us, length us, event | category | flops | bytes accessed | tf_op | source)
XLA Modules:
  0.0 788.9 jit_solution(10721165272953729870)
XLA Ops:
  8.6 25.4 %all_gather.12 = bf16[1024,256]{1,0:T(8,128)(2,1)S(1)} all-gather(bf16[64,256]{1,0:T(8,128)(2,1)} %param.22), channel_id=1, replica_groups=mesh['row'=8,'col'=16] {'col'}, dimensions={0}, use_global_device_ids=true | all-gather | bytes 557056 | tf_op jit(solution)/shard_map/all_gather | solution.py:99
  42.9 12.5 %all-reduce = f32[1024]{0:T(1024)S(1)} all-reduce(f32[1024]{0:T(1024)S(1)} %fusion.5), channel_id=3, replica_groups=mesh['row'=8,'col'=16] {'row'}, use_global_device_ids=true, to_apply=%region_2.0.clone | all-reduce | flops 1024 | bytes 8192
  60.8 5.6 reduce-scatter.25.cloned.1.call-done
  69.0 31.3 %reduce-scatter.15.cloned.1.call-done = f32[128,256]{1,0:T(8,128)} async-done(((f32[1024,256]{1,0:T(8,128)}), f32[128,256]{1,0:T(8,128)}) %reduce-scatter.15.cloned.1.call-update) | async-done | bytes 131088 | tf_op jit(solution)/shard_map/reduce_scatter | solution.py:113
  102.1 33.8 %reduce-scatter.13.cloned.1.call-done = f32[128,512]{1,0:T(8,128)} async-done(((f32[1024,512]{1,0:T(8,128)}), f32[128,512]{1,0:T(8,128)}) %reduce-scatter.13.cloned.1.call-update) | async-done | bytes 262160 | tf_op jit(solution)/shard_map/reduce_scatter | solution.py:111
  137.4 5.4 broadcast.153.clone2
  142.7 103.3 %while.28 = (s32[]{:T(128)}, f32[8,4,64,128]{3,2,1,0:T(8,128)S(1)}, f32[16,8,4,64]{3,2,1,0:T(4,128)S(1)}, bf16[16,8,4,64,128]{4,3,2,0,1:T(8,128)(2,1)}, f32[16,8...) while((s32[]{:T(128)}, f32[8,4,64,128]{3,2,1,0:T(8,128)S(1)}, ...), condition=%wide.region_6.0_spmd, body=%wide.region_5.0_spmd.sunk | while | flops 4200450 | bytes 3777949 | solution.py:40
  246.5 40.5 %psum.14 = f32[128]{0:T(128)S(1)} all-reduce(f32[128]{0:T(128)S(1)} %get-tuple-element.179), channel_id=1, replica_groups=mesh['row'=8,'col'=16] {'col'}, use_global_device_ids=true, to_apply=%region_8.9 | all-reduce | flops 128 | bytes 1024 | tf_op jit(solution)/shard_map/psum | solution.py:145
  287.8 13.1 %all_gather.13 = bf16[1024,256]{1,0:T(8,128)(2,1)S(1)} all-gather(bf16[128,256]{1,0:T(8,128)(2,1)S(1)} %multiply_convert_fusion.1), channel_id=1, replica_groups=mesh['row'=8,'col'=16] {'row'}, dimensions={0}, use_global_device_ids=true | all-gather | bytes 589824 | tf_op jit(solution)/shard_map/all_gather | solution.py:153
  302.9 67.3 %reduce-scatter.17.cloned.1.call-done = bf16[64,256]{1,0:T(8,128)(2,1)} async-done(((bf16[1024,256]{1,0:T(8,128)(2,1)}), bf16[64,256]{1,0:T(8,128)(2,1)}) %reduce-scatter.17.cloned.1.call-update) | async-done | bytes 32784 | tf_op jit(solution)/shard_map/reduce_scatter | solution.py:157
  371.0 23.3 %all_gather.14 = bf16[1024,256]{1,0:T(8,128)(2,1)S(1)} all-gather(bf16[64,256]{1,0:T(8,128)(2,1)S(1)} %add_convert_fusion.1), channel_id=1, replica_groups=mesh['row'=8,'col'=16] {'col'}, dimensions={0}, use_global_device_ids=true | all-gather | bytes 557056 | tf_op jit(solution)/shard_map/all_gather | solution.py:99
  400.6 13.3 %reshape.291 = bf16[128,32768]{1,0:T(8,128)(2,1)} reshape(bf16[8,16,4,64,128]{4,3,2,1,0:T(8,128)(2,1)} %bitcast.249) | data formatting | bytes 16777216 | tf_op jit(solution)/shard_map/reshape | solution.py:163
  420.7 12.6 %all-reduce.1 = f32[1024]{0:T(1024)S(1)} all-reduce(f32[1024]{0:T(1024)S(1)} %fusion.7), channel_id=8, replica_groups=mesh['row'=8,'col'=16] {'row'}, use_global_device_ids=true, to_apply=%region_12.13.clone | all-reduce | flops 1024 | bytes 8192
  434.7 24.2 %reduce-scatter.21.cloned.1.call-done = f32[128,256]{1,0:T(8,128)} async-done(((f32[1024,256]{1,0:T(8,128)}), f32[128,256]{1,0:T(8,128)}) %reduce-scatter.21.cloned.1.call-update) | async-done | bytes 131088 | tf_op jit(solution)/shard_map/reduce_scatter | solution.py:113
  460.1 34.4 %reduce-scatter.19.cloned.1.call-done = f32[128,512]{1,0:T(8,128)} async-done(((f32[1024,512]{1,0:T(8,128)}), f32[128,512]{1,0:T(8,128)}) %reduce-scatter.19.cloned.1.call-update) | async-done | bytes 262160 | tf_op jit(solution)/shard_map/reduce_scatter | solution.py:111
  496.0 5.4 broadcast.153.clone
  501.4 70.9 %while.29 = (s32[]{:T(128)}, f32[8,4,64,128]{3,2,1,0:T(8,128)S(1)}, f32[16,8,4,64]{3,2,1,0:T(4,128)S(1)}, bf16[16,8,4,64,128]{4,3,2,0,1:T(8,128)(2,1)}, f32[16,8...) while((s32[]{:T(128)}, f32[8,4,64,128]{3,2,1,0:T(8,128)S(1)}, ...), condition=%wide.region_16.17_spmd, body=%wide.region_15.16_spmd.sunk | while | flops 4200450 | bytes 3778445 | solution.py:40
  572.4 13.3 %reshape.292 = bf16[128,32768]{1,0:T(8,128)(2,1)} reshape(bf16[8,16,4,64,128]{4,3,2,1,0:T(8,128)(2,1)} %bitcast.247) | data formatting | bytes 16777216 | tf_op jit(solution)/shard_map/reshape | solution.py:163
  593.3 7.0 all-to-all-start
  600.8 81.9 %psum.15 = f32[128]{0:T(128)S(1)} all-reduce(f32[128]{0:T(128)S(1)} %get-tuple-element.177), channel_id=1, replica_groups=mesh['row'=8,'col'=16] {'col'}, use_global_device_ids=true, to_apply=%region_18.19 | all-reduce | flops 128 | bytes 1024 | tf_op jit(solution)/shard_map/psum | solution.py:145
  682.8 21.8 %all_gather.15 = bf16[1024,256]{1,0:T(8,128)(2,1)S(1)} all-gather(bf16[128,256]{1,0:T(8,128)(2,1)S(1)} %multiply_convert_fusion), channel_id=1, replica_groups=mesh['row'=8,'col'=16] {'row'}, dimensions={0}, use_global_device_ids=true | all-gather | bytes 589824 | tf_op jit(solution)/shard_map/all_gather | solution.py:153
  705.7 13.8 %pad_maximum_fusion = bf16[2,8,16,4,64,128]{5,4,3,2,1,0:T(8,128)(2,1)} fusion(bf16[1,8,16,4,64,128]{5,4,3,2,1,0:T(8,128)(2,1)} %bitcast.248, bf16[1,8,16,4,64,128]{5,4,3,2,1,0:T(8,128)(2,1)} %bitcast.250), kind=kLoop, calls=%fused_computation.22 | loop fusion | flops 8388608 | bytes 33554432 | tf_op jit(solution)/shard_map/stack | solution.py:174
  719.5 55.1 %reduce-scatter.23.cloned.1.call-done = bf16[64,256]{1,0:T(8,128)(2,1)} async-done(((bf16[1024,256]{1,0:T(8,128)(2,1)}), bf16[64,256]{1,0:T(8,128)(2,1)}) %reduce-scatter.23.cloned.1.call-update) | async-done | bytes 32784 | tf_op jit(solution)/shard_map/reduce_scatter | solution.py:157
  776.1 6.0 copy.143
  (447 shorter events, 225.7 us)
Async XLA Ops:
  7.2 50.6 %copy-start.9 = (f32[2,4,256]{2,1,0:T(4,128)S(1)}, f32[2,4,256]{2,1,0:T(4,128)}, u32[]{:S(2)}) copy-start(f32[2,4,256]{2,1,0:T(4,128)} %param.28) | copy-start | bytes 24580
  7.2 51.2 %copy-start.5 = (bf16[2,8,3,256]{3,1,2,0:T(8,128)(2,1)S(1)}, bf16[2,8,3,256]{3,1,2,0:T(8,128)(2,1)}, u32[]{:S(2)}) copy-start(bf16[2,8,3,256]{3,1,2,0:T(8,128)(2,1)} %param.34) | copy-start | bytes 73732
  7.3 51.2 %copy-start.6 = (bf16[2,8,3,256]{3,1,2,0:T(8,128)(2,1)S(1)}, bf16[2,8,3,256]{3,1,2,0:T(8,128)(2,1)}, u32[]{:S(2)}) copy-start(bf16[2,8,3,256]{3,1,2,0:T(8,128)(2,1)} %param.35) | copy-start | bytes 73732
  7.3 59.2 %reduce-scatter.25.cloned.1.call-start = ((), (), s32[]{:S(2)}) async-start(), calls=%async_computation.15 | async-start | bytes 589824
  35.9 64.4 %reduce-scatter.15.cloned.1.call-start = ((), (), s32[]{:S(2)}) async-start(), calls=%async_computation.10 | async-start | bytes 1179648 | tf_op jit(solution)/shard_map/reduce_scatter | solution.py:113
  38.1 97.8 %reduce-scatter.13.cloned.1.call-start = ((), (), s32[]{:S(2)}) async-start(), calls=%async_computation.9 | async-start | bytes 2359296 | tf_op jit(solution)/shard_map/reduce_scatter | solution.py:111
  41.4 328.8 %reduce-scatter.17.cloned.1.call-start = ((), (), s32[]{:S(2)}) async-start(), calls=%async_computation.11 | async-start | bytes 557056 | tf_op jit(solution)/shard_map/reduce_scatter | solution.py:157
  142.7 227.5 %copy-start.3 = (bf16[64,256]{1,0:T(8,128)(2,1)S(1)}, bf16[64,256]{1,0:T(8,128)(2,1)}, u32[]{:S(2)}) copy-start(bf16[64,256]{1,0:T(8,128)(2,1)} %param.22) | copy-start | bytes 98308
  142.7 253.4 %copy-start.1 = (bf16[2,256,256]{2,1,0:T(8,128)(2,1)S(1)}, bf16[2,256,256]{2,1,0:T(8,128)(2,1)}, u32[]{:S(2)}) copy-start(bf16[2,256,256]{2,1,0:T(8,128)(2,1)} %param.25) | copy-start | bytes 786436
  246.1 152.2 %copy-start.7 = (f32[1,256]{1,0:T(1,128)S(1)}, f32[1,256]{1,0:T(1,128)}, u32[]{:S(2)}) copy-start(f32[1,256]{1,0:T(1,128)} %get-tuple-element.219) | copy-start | bytes 3076
  246.1 154.0 %copy-start.27 = (s32[8]{0:T(128)S(1)}, s32[8]{0:T(128)}, u32[]{:S(2)}) copy-start(s32[8]{0:T(128)} %param.38) | copy-start | bytes 100
  246.1 154.2 %copy-start.23 = (s32[4,2]{0,1:T(2,128)S(1)}, s32[4,2]{0,1:T(2,128)}, u32[]{:S(2)}) copy-start(s32[4,2]{0,1:T(2,128)} %param.39) | copy-start | bytes 100
  246.1 154.3 %copy-start.26 = (s32[8]{0:T(128)S(1)}, s32[8]{0:T(128)}, u32[]{:S(2)}) copy-start(s32[8]{0:T(128)} %param.37) | copy-start | bytes 100
  302.9 130.5 %reduce-scatter.27.cloned.1.call-start = ((), (), s32[]{:S(2)}) async-start(), calls=%async_computation.16 | async-start | bytes 589824
  396.1 62.8 %reduce-scatter.21.cloned.1.call-start = ((), (), s32[]{:S(2)}) async-start(), calls=%async_computation.13 | async-start | bytes 1179648 | tf_op jit(solution)/shard_map/reduce_scatter | solution.py:113
  398.2 96.4 %reduce-scatter.19.cloned.1.call-start = ((), (), s32[]{:S(2)}) async-start(), calls=%async_computation.12 | async-start | bytes 2359296 | tf_op jit(solution)/shard_map/reduce_scatter | solution.py:111
  414.0 81.8 %copy-start.10 = (f32[1,1,256]{2,1,0:T(1,128)S(1)}, f32[1,1,256]{2,1,0:T(1,128)}, u32[]{:S(2)}) copy-start(f32[1,1,256]{2,1,0:T(1,128)} %get-tuple-element.209) | copy-start | bytes 3076
  414.0 81.8 %copy-start.11 = (f32[1,1,256]{2,1,0:T(1,128)S(1)}, f32[1,1,256]{2,1,0:T(1,128)}, u32[]{:S(2)}) copy-start(f32[1,1,256]{2,1,0:T(1,128)} %get-tuple-element.210) | copy-start | bytes 3076
  414.0 81.8 %copy-start.12 = (f32[1,1,256]{2,1,0:T(1,128)S(1)}, f32[1,1,256]{2,1,0:T(1,128)}, u32[]{:S(2)}) copy-start(f32[1,1,256]{2,1,0:T(1,128)} %get-tuple-element.215) | copy-start | bytes 3076
  414.0 81.8 %copy-start.13 = (f32[1,1,256]{2,1,0:T(1,128)S(1)}, f32[1,1,256]{2,1,0:T(1,128)}, u32[]{:S(2)}) copy-start(f32[1,1,256]{2,1,0:T(1,128)} %get-tuple-element.216) | copy-start | bytes 3076
  590.9 91.8 %copy-start.18 = (f32[1,256]{1,0:T(1,128)S(1)}, f32[1,256]{1,0:T(1,128)}, u32[]{:S(2)}) copy-start(f32[1,256]{1,0:T(1,128)} %get-tuple-element.217) | copy-start | bytes 3076
  590.9 113.7 %copy-start.2 = (bf16[2,256,256]{2,1,0:T(8,128)(2,1)S(1)}, bf16[2,256,256]{2,1,0:T(8,128)(2,1)}, u32[]{:S(2)}) copy-start(bf16[2,256,256]{2,1,0:T(8,128)(2,1)} %param.33) | copy-start | bytes 786436
  593.3 182.7 %all-to-all-start = ((bf16[16,2,2,4,64,128]{5,4,3,1,2,0:T(8,128)(2,1)}), bf16[16,2,2,4,64,128]{5,4,3,1,2,0:T(8,128)(2,1)}, u32[]{:S(2)}, u32[]{:S(2)}) async-start(bf16[16,2,2,4,64,128]{5,4,3,1,2,0:T(8,128)(2,1)} %pad_maximum_fusion.1), calls=%async_computation.6 | async-start | bytes 8388608 | tf_op jit(solution)/shard_map/all_to_all | solution.py:170
  600.3 174.4 %reduce-scatter.23.cloned.1.call-start = ((), (), s32[]{:S(2)}) async-start(), calls=%async_computation.14 | async-start | bytes 557056 | tf_op jit(solution)/shard_map/reduce_scatter | solution.py:157
  (14 other events, 557.1 us)
Sparse Core Ops, SparseCore 0:
  36.0 30.4 reduce-scatter.24
  69.5 30.7 reduce-scatter.14
  103.4 32.4 reduce-scatter.12
  303.0 67.1 reduce-scatter.16
  396.2 29.5 reduce-scatter.26
  428.2 30.6 reduce-scatter.20
  462.0 32.5 reduce-scatter.18
  705.8 68.7 reduce-scatter.22
where the time goes:
time: 792 us; the launch traced here: 789 us
  waiting for transfers between devices  252 us (32%)
  blocking collectives  231 us (29%)
  matrix products  105 us (13%)
  other arithmetic  90.8 us (11%)
  local copies, waits for them, and re-layouts  86.9 us (11%)
  between operations  15.4 us (2%)
    psum x2, blocking collectives, local(): gate_square = lax.psum(jnp.sum(gated_raw * gated_raw, axis=1), 'col')  122 us
    reduce_scatter x2, waiting for transfers between devices, local(): lax.psum_scatter(partial_out.astype(jnp.bfloat16), 'col', scatter_dimensi...  122 us
    dot_general x32, matrix products, advance(): jnp.einsum('rhpn,rn->rhp', updated, c_now, precision=lax.Precision.HIGHEST)  80.9 us
    reduce_scatter x2, waiting for transfers between devices, local(): lax.psum_scatter(inner_part, 'row', scatter_dimension=0, tiled=True)  68.3 us
    dynamic_update_slice x64, other arithmetic, ssm_scan(): last_state, (outputs, states) = lax.scan(advance, start_state, time_major)  62.7 us
    reduce_scatter x2, waiting for transfers between devices, local(): lax.psum_scatter(proj_part, 'row', scatter_dimension=0, tiled=True)  55.6 us
    all_gather x2, blocking collectives, local(): all_tokens = lax.all_gather(hidden, 'col', axis=0, tiled=True)  48.8 us
    all_gather x2, blocking collectives, local(): lax.all_gather(gated, 'row', axis=0, tiled=True)  34.9 us
  transfers between devices with their start and end apart: 9, of which 7 were waited for; matrix products, arithmetic and copies ran while one was open for 8% of the time, Pallas kernels for 0%

commit v1 on v0

--- a/solution.py
+++ b/solution.py
@@ -96,7 +96,17 @@
     step_outputs = []
     chosen_layers = []
     for layer_index in range(layer_count):
-        all_tokens = lax.all_gather(hidden, "col", axis=0, tiled=True)
+        k_all = jax.lax.axis_size("col")
+        oldest = hidden
+        kept_arr = sorted(((ii, (ii + 1) % k_all) for ii in range(k_all)))
+        j = 1
+        so_far_all = [oldest]
+        while j < k_all:
+            oldest = jax.lax.ppermute(oldest, "col", kept_arr)
+            so_far_all.insert(0, oldest)
+            j += 1
+        mixed_arr = jnp.concatenate(so_far_all, 0)
+        all_tokens = jnp.roll(mixed_arr, (jax.lax.axis_index("col") + 1) * hidden.shape[0], 0)
         tokens_f = all_tokens.astype(jnp.float32)
         scaled = (tokens_f * input_gain[layer_index]).astype(jnp.bfloat16)
         square_part = jnp.sum(tokens_f * tokens_f, axis=1)

time: 792 us -> 1020 us (1.29)
  waiting for transfers between devices: 252 us -> 462 us
  blocking collectives: 231 us -> 182 us
  local copies, waits for them, and re-layouts: 86.9 us -> 122 us
  other arithmetic: 90.8 us -> 114 us
    ppermute x0 -> x30, waiting for transfers between devices: none -> 215 us  [local(): oldest = jax.lax.ppermute(oldest, 'col', kept_arr)]
    all_gather x2 -> x0, blocking collectives: 48.8 us -> none  [local(): all_tokens = lax.all_gather(hidden, 'col', axis=0, tiled=True)]
    mul x32, other arithmetic: 2.37 us -> 13.8 us  [advance(): delta_now[:, :, None] * value_now]
    dynamic_slice x32, local copies, waits for them, and re-layouts: 0.05 us -> 11 us  [ssm_scan(): last_state, (outputs, states) = lax.scan(advance, start_state, time_major)]
    mul x64, local copies, waits for them, and re-layouts: 13.8 us -> 24.7 us  [advance(): delta_now[:, :, None] * value_now]
    mul x32, local copies, waits for them, and re-layouts: 11.3 us -> 22 us  [advance(): (delta_now[:, :, None] * value_now)[:, :, :, None] * b_now[:, None, None, :]]
  transfers between devices with their start and end apart: 9 -> 39, of which waited for: 7 -> 37; matrix products, arithmetic and copies ran while one was open for 8% -> 6% of each run, Pallas kernels for 0% -> 0%
where the time goes in v1:
time: 1020 us; the launch traced here: 1010 us
  waiting for transfers between devices  462 us (45%)
  blocking collectives  182 us (18%)
  local copies, waits for them, and re-layouts  122 us (12%)
  other arithmetic  114 us (11%)
  matrix products  103 us (10%)
  between operations  15.6 us (2%)
    ppermute x30, waiting for transfers between devices, local(): oldest = jax.lax.ppermute(oldest, 'col', kept_arr)  215 us
    psum x2, blocking collectives, local(): gate_square = lax.psum(jnp.sum(gated_raw * gated_raw, axis=1), 'col')  123 us
    reduce_scatter x2, waiting for transfers between devices, local(): lax.psum_scatter(partial_out.astype(jnp.bfloat16), 'col', scatter_dimensi...  122 us
    dot_general x32, matrix products, advance(): jnp.einsum('rhpn,rn->rhp', updated, c_now, precision=lax.Precision.HIGHEST)  80.9 us
    dynamic_update_slice x64, other arithmetic, ssm_scan(): last_state, (outputs, states) = lax.scan(advance, start_state, time_major)  72.6 us
    reduce_scatter x2, waiting for transfers between devices, local(): lax.psum_scatter(inner_part, 'row', scatter_dimension=0, tiled=True)  67.6 us
    reduce_scatter x2, waiting for transfers between devices, local(): lax.psum_scatter(proj_part, 'row', scatter_dimension=0, tiled=True)  54.4 us
    all_gather x2, blocking collectives, local(): lax.all_gather(gated, 'row', axis=0, tiled=True)  34.6 us
  transfers between devices with their start and end apart: 39, of which 37 were waited for; matrix products, arithmetic and copies ran while one was open for 6% of the time, Pallas kernels for 0%

profile of v1, /device:TPU:0, one launch (start us, length us, event | category | flops | bytes accessed | tf_op | source)
XLA Modules:
  0.0 1009.4 jit_solution(4031153861265545026)
XLA Ops:
  15.8 7.2 collective-permute-done.1
  23.0 7.2 collective-permute-done.2
  30.3 7.2 collective-permute-done.3
  37.5 7.2 collective-permute-done.4
  44.7 7.2 collective-permute-done.5
  80.9 7.4 collective-permute-done.10
  133.6 12.6 %all-reduce = f32[1024]{0:T(1024)S(1)} all-reduce(f32[1024]{0:T(1024)S(1)} %get-tuple-element.184), channel_id=3, replica_groups=mesh['row'=8,'col'=16] {'row'}, use_global_device_ids=true, to_apply=%region_2.4.clone | all-reduce | flops 1024 | bytes 8192
  150.9 31.3 %reduce-scatter.15.cloned.1.call-done = f32[128,256]{1,0:T(8,128)} async-done(((f32[1024,256]{1,0:T(8,128)}), f32[128,256]{1,0:T(8,128)}) %reduce-scatter.15.cloned.1.call-update) | async-done | bytes 131088 | tf_op jit(solution)/shard_map/reduce_scatter | solution.py:123
  184.1 33.9 %reduce-scatter.13.cloned.1.call-done = f32[128,512]{1,0:T(8,128)} async-done(((f32[1024,512]{1,0:T(8,128)}), f32[128,512]{1,0:T(8,128)}) %reduce-scatter.13.cloned.1.call-update) | async-done | bytes 262160 | tf_op jit(solution)/shard_map/reduce_scatter | solution.py:121
  224.8 92.4 %while.28 = (s32[]{:T(128)}, f32[8,4,64,128]{3,2,1,0:T(8,128)S(1)}, f32[16,8,4,64]{3,2,1,0:T(4,128)S(1)}, bf16[16,8,4,64,128]{4,3,2,0,1:T(8,128)(2,1)}, f32[16,8...) while((s32[]{:T(128)}, f32[8,4,64,128]{3,2,1,0:T(8,128)S(1)}, ...), condition=%wide.region_6.8_spmd, body=%wide.region_5.7_spmd.sunk | while | flops 4200450 | bytes 3778445 | solution.py:40
  317.6 40.5 %psum.14 = f32[128]{0:T(128)S(1)} all-reduce(f32[128]{0:T(128)S(1)} %get-tuple-element.182), channel_id=1, replica_groups=mesh['row'=8,'col'=16] {'col'}, use_global_device_ids=true, to_apply=%region_8.10 | all-reduce | flops 128 | bytes 1024 | tf_op jit(solution)/shard_map/psum | solution.py:155
  358.3 13.1 %all_gather.6 = bf16[1024,256]{1,0:T(8,128)(2,1)S(1)} all-gather(bf16[128,256]{1,0:T(8,128)(2,1)S(1)} %multiply_convert_fusion.1), channel_id=1, replica_groups=mesh['row'=8,'col'=16] {'row'}, dimensions={0}, use_global_device_ids=true | all-gather | bytes 589824 | tf_op jit(solution)/shard_map/all_gather | solution.py:163
  373.5 67.3 %reduce-scatter.17.cloned.1.call-done = bf16[64,256]{1,0:T(8,128)(2,1)} async-done(((bf16[1024,256]{1,0:T(8,128)(2,1)}), bf16[64,256]{1,0:T(8,128)(2,1)}) %reduce-scatter.17.cloned.1.call-update) | async-done | bytes 32784 | tf_op jit(solution)/shard_map/reduce_scatter | solution.py:167
  463.3 7.5 collective-permute-done.18
  556.5 13.3 %reshape.291 = bf16[128,32768]{1,0:T(8,128)(2,1)} reshape(bf16[8,16,4,64,128]{4,3,2,1,0:T(8,128)(2,1)} %bitcast.249) | data formatting | bytes 16777216 | tf_op jit(solution)/shard_map/reshape | solution.py:173
  575.0 12.4 %all-reduce.1 = f32[1024]{0:T(1024)S(1)} all-reduce(f32[1024]{0:T(1024)S(1)} %get-tuple-element.180), channel_id=8, replica_groups=mesh['row'=8,'col'=16] {'row'}, use_global_device_ids=true, to_apply=%region_12.14.clone | all-reduce | flops 1024 | bytes 8192
  590.0 23.1 %reduce-scatter.21.cloned.1.call-done = f32[128,256]{1,0:T(8,128)} async-done(((f32[1024,256]{1,0:T(8,128)}), f32[128,256]{1,0:T(8,128)}) %reduce-scatter.21.cloned.1.call-update) | async-done | bytes 131088 | tf_op jit(solution)/shard_map/reduce_scatter | solution.py:123
  615.0 33.7 %reduce-scatter.19.cloned.1.call-done = f32[128,512]{1,0:T(8,128)} async-done(((f32[1024,512]{1,0:T(8,128)}), f32[128,512]{1,0:T(8,128)}) %reduce-scatter.19.cloned.1.call-update) | async-done | bytes 262160 | tf_op jit(solution)/shard_map/reduce_scatter | solution.py:121
  657.8 135.6 %while.29 = (s32[]{:T(128)}, f32[8,4,64,128]{3,2,1,0:T(8,128)S(1)}, f32[16,8,4,64]{3,2,1,0:T(4,128)}, bf16[16,8,4,64,128]{4,3,2,0,1:T(8,128)(2,1)}, f32[16,8,4]{...) while((s32[]{:T(128)}, f32[8,4,64,128]{3,2,1,0:T(8,128)S(1)}, ...), condition=%wide.region_16.18_spmd, body=%wide.region_15.17_spmd.sunk | while | flops 4200450 | bytes 3769757 | solution.py:40
  793.4 13.3 %reshape.292 = bf16[128,32768]{1,0:T(8,128)(2,1)} reshape(bf16[8,16,4,64,128]{4,3,2,1,0:T(8,128)(2,1)} %bitcast.247) | data formatting | bytes 16777216 | tf_op jit(solution)/shard_map/reshape | solution.py:173
  821.6 82.0 %psum.15 = f32[128]{0:T(128)S(1)} all-reduce(f32[128]{0:T(128)S(1)} %get-tuple-element.178), channel_id=1, replica_groups=mesh['row'=8,'col'=16] {'col'}, use_global_device_ids=true, to_apply=%region_18.20 | all-reduce | flops 128 | bytes 1024 | tf_op jit(solution)/shard_map/psum | solution.py:155
  903.7 21.5 %all_gather.7 = bf16[1024,256]{1,0:T(8,128)(2,1)S(1)} all-gather(bf16[128,256]{1,0:T(8,128)(2,1)S(1)} %multiply_convert_fusion), channel_id=1, replica_groups=mesh['row'=8,'col'=16] {'row'}, dimensions={0}, use_global_device_ids=true | all-gather | bytes 589824 | tf_op jit(solution)/shard_map/all_gather | solution.py:163
  926.3 13.8 %pad_maximum_fusion = bf16[2,8,16,4,64,128]{5,4,3,2,1,0:T(8,128)(2,1)} fusion(bf16[1,8,16,4,64,128]{5,4,3,2,1,0:T(8,128)(2,1)} %bitcast.248, bf16[1,8,16,4,64,128]{5,4,3,2,1,0:T(8,128)(2,1)} %bitcast.250), kind=kLoop, calls=%fused_computation.22 | loop fusion | flops 8388608 | bytes 33554432 | tf_op jit(solution)/shard_map/stack | solution.py:184
  940.1 55.1 %reduce-scatter.23.cloned.1.call-done = bf16[64,256]{1,0:T(8,128)(2,1)} async-done(((bf16[1024,256]{1,0:T(8,128)(2,1)}), bf16[64,256]{1,0:T(8,128)(2,1)}) %reduce-scatter.23.cloned.1.call-update) | async-done | bytes 32784 | tf_op jit(solution)/shard_map/reduce_scatter | solution.py:167
  (535 shorter events, 475.5 us)
Async XLA Ops:
  7.3 141.2 %reduce-scatter.25.cloned.1.call-start = ((), (), s32[]{:S(2)}) async-start(), calls=%async_computation.15 | async-start | bytes 589824
  7.3 8.5 collective-permute-start
  15.8 7.2 collective-permute-start.1
  23.0 7.2 collective-permute-start.2
  30.3 7.2 collective-permute-start.3
  44.7 7.2 collective-permute-start.5
  52.0 7.2 collective-permute-start.6
  59.2 7.2 collective-permute-start.7
  66.4 7.2 collective-permute-start.8
  73.7 7.2 collective-permute-start.9
  80.9 7.4 collective-permute-start.10
  88.3 7.2 collective-permute-start.11
  95.6 7.2 collective-permute-start.12
  121.0 61.3 %reduce-scatter.15.cloned.1.call-start = ((), (), s32[]{:S(2)}) async-start(), calls=%async_computation.10 | async-start | bytes 1179648 | tf_op jit(solution)/shard_map/reduce_scatter | solution.py:123
  123.2 94.8 %reduce-scatter.13.cloned.1.call-start = ((), (), s32[]{:S(2)}) async-start(), calls=%async_computation.9 | async-start | bytes 2359296 | tf_op jit(solution)/shard_map/reduce_scatter | solution.py:121
  126.5 314.2 %reduce-scatter.17.cloned.1.call-start = ((), (), s32[]{:S(2)}) async-start(), calls=%async_computation.11 | async-start | bytes 557056 | tf_op jit(solution)/shard_map/reduce_scatter | solution.py:167
  373.4 214.1 %reduce-scatter.27.cloned.1.call-start = ((), (), s32[]{:S(2)}) async-start(), calls=%async_computation.16 | async-start | bytes 589824
  441.5 7.3 collective-permute-start.15
  463.3 7.5 collective-permute-start.18
  543.1 7.2 collective-permute-start.29
  552.6 60.5 %reduce-scatter.21.cloned.1.call-start = ((), (), s32[]{:S(2)}) async-start(), calls=%async_computation.13 | async-start | bytes 1179648 | tf_op jit(solution)/shard_map/reduce_scatter | solution.py:123
  554.0 94.6 %reduce-scatter.19.cloned.1.call-start = ((), (), s32[]{:S(2)}) async-start(), calls=%async_computation.12 | async-start | bytes 2359296 | tf_op jit(solution)/shard_map/reduce_scatter | solution.py:121
  814.2 182.4 %all-to-all-start = ((bf16[16,2,2,4,64,128]{5,4,3,1,2,0:T(8,128)(2,1)}), bf16[16,2,2,4,64,128]{5,4,3,1,2,0:T(8,128)(2,1)}, u32[]{:S(2)}, u32[]{:S(2)}) async-start(bf16[16,2,2,4,64,128]{5,4,3,1,2,0:T(8,128)(2,1)} %pad_maximum_fusion.1), calls=%async_computation.6 | async-start | bytes 8388608 | tf_op jit(solution)/shard_map/all_to_all | solution.py:180
  821.2 174.1 %reduce-scatter.23.cloned.1.call-start = ((), (), s32[]{:S(2)}) async-start(), calls=%async_computation.14 | async-start | bytes 557056 | tf_op jit(solution)/shard_map/reduce_scatter | solution.py:167
  (43 other events, 3469.9 us)
Sparse Core Ops, SparseCore 0:
  121.1 27.3 reduce-scatter.24
  151.5 30.6 reduce-scatter.14
  185.4 32.5 reduce-scatter.12
  373.5 67.1 reduce-scatter.16
  552.8 27.2 reduce-scatter.26
  582.4 30.6 reduce-scatter.20
  616.2 32.4 reduce-scatter.18
  926.4 68.7 reduce-scatter.22
